TPU v7x, 32 devices: a whole 2x2x4 slice. The times are simulated.
32 devices in a mesh: row: 4 (over y, x), col: 8 (over z, core).
Axes of the slice: x: 2, y: 2, z: 4, core: 2. Of those that a mesh axis runs over, the one named last changes fastest.
Arguments:
- momentum: float32 [4608, 8192], P('row', 'col'), may hold values from -37 to 37
Outputs:
- update: float32 [4608, 8192], P('row', 'col')
All inputs are finite; a program needn't handle non-finite values.
Results may differ from a plain program's by a relative error of at most 0.0049.
Values may be sent and summed in bfloat16 or wider, within the bound.
No kernel may reach another device: no remote copies, remote signals or barrier semaphores. Data moves between devices by JAX's collectives and lax.ppermute only.
A program may use at most 128 MiB of HBM per device.

v0:
```python
import math
import jax
import jax.numpy as jnp
from jax import lax
from jax.sharding import PartitionSpec as P

ROWS = 4608
COLS = 8192
quintic_a = 3.4445
quintic_b = -4.775
quintic_c = 2.0315


def from_root(shard, axis, root):
    mine = lax.axis_index(axis) == root
    return lax.psum(jnp.where(mine, shard, jnp.zeros_like(shard)), axis)


def rows_product(left, right):
    return lax.dot_general(
        left, right, (((1,), (1,)), ((), ())), preferred_element_type=jnp.float32
    )


def body(momentum):
    partial_sum = jnp.sum(momentum * momentum)
    norm_squares = lax.psum(partial_sum, ("row", "col"))
    factor = 0.6 * math.sqrt(ROWS) / (jnp.sqrt(norm_squares) + 1e-07)
    scaled = (momentum * factor).astype(jnp.bfloat16)
    tile_ratio = lax.axis_size("col") // lax.axis_size("row")
    col_index = lax.axis_index("col")
    source_row = col_index // tile_ratio
    half_index = col_index % tile_ratio
    row_panel = lax.all_gather(scaled, "col", axis=1, tiled=True)
    part_rows = row_panel.shape[0] // tile_ratio
    own_part = lax.dynamic_slice_in_dim(row_panel, half_index * part_rows, part_rows, 0)
    peer_rows = from_root(own_part, "row", source_row)
    gram = rows_product(row_panel, peer_rows).astype(jnp.bfloat16)
    gram_panel = lax.all_gather(gram, "col", axis=1, tiled=True)
    gram_columns = lax.all_gather(gram, "row", axis=0, tiled=True)
    squared = jnp.dot(gram_panel, gram_columns, preferred_element_type=jnp.float32)
    poly = (quintic_b * gram.astype(jnp.float32) + quintic_c * squared).astype(jnp.bfloat16)
    poly_panel = lax.all_gather(poly, "col", axis=1, tiled=True)
    product = jnp.dot(
        poly_panel,
        lax.all_gather(scaled, "row", axis=0, tiled=True),
        preferred_element_type=jnp.float32,
    )
    return math.sqrt(COLS) * (quintic_a * scaled.astype(jnp.float32) + product)


def solution(mesh):
    placed = (P("row", "col"),)
    return jax.shard_map(
        body, mesh=mesh, in_specs=placed, out_specs=P("row", "col"), check_vma=False
    )
```

profile of v0, /device:TPU:0, one launch (start us, length us, event | category | flops | bytes accessed | tf_op | source)
XLA Modules:
  0.0 828.4 jit_solution(4937114119938713192)
XLA Ops:
  6.5 0.0 all-gather.6.cloned.1.call-start
  6.5 4.2 multiply_reduce_fusion
  10.7 42.2 %psum.14 = f32[]{:T(128)} all-reduce(f32[]{:T(128)} %multiply_reduce_fusion), channel_id=1, replica_groups=mesh['row'=4,'col'=8] {'row','col'}, use_global_device_ids=true, to_apply=%region_1.0 | all-reduce | flops 1 | bytes 8 | tf_op jit(solution)/shard_map/psum | solution.py:27
  53.6 4.4 multiply_convert_fusion
  58.0 0.0 all-gather.6.cloned.1.call-update
  58.0 0.0 all-reduce.2.cloned.1.call-start
  58.1 168.3 %all-gather.6.cloned.1.call-done = bf16[1152,8192]{1,0:T(8,128)(2,1)} async-done(((bf16[1152,1024]{1,0:T(8,128)(2,1)}), bf16[1152,8192]{1,0:T(8,128)(2,1)}) %all-gather.6.cloned.1.call-update) | async-done | bytes 18874384 | tf_op jit(solution)/shard_map/all_gather | solution.py:34
  226.5 9.8 %dynamic-slice_select_fusion = bf16[576,8192]{1,0:T(8,128)(2,1)} fusion(bf16[1152,8192]{1,0:T(8,128)(2,1)} %all-gather.6.cloned.1.call-done, s32[]{:T(128)S(6)} %select_n.25, pred[]{:T(512)S(6)} %eq.5), kind=kLoop, calls=%fused_computation | loop fusion | flops 4718592 | bytes 18874372 | tf_op jit(solution)/shard_map/jit(_where)/select_n | solution.py:16
  236.2 0.0 all-reduce.2.cloned.1.call-update
  236.2 0.0 all-gather.10.cloned.1.call-start
  236.3 186.7 %all-reduce.2.cloned.1.call-done = bf16[576,8192]{1,0:T(8,128)(2,1)} async-done(((bf16[576,8192]{1,0:T(8,128)(2,1)}), bf16[576,8192]{1,0:T(8,128)(2,1)}) %all-reduce.2.cloned.1.call-update) | async-done | bytes 9437200 | tf_op jit(solution)/shard_map/psum | solution.py:16
  423.0 18.8 %convolution_convert_fusion = bf16[1152,576]{0,1:T(8,128)(2,1)} fusion(bf16[1152,8192]{1,0:T(8,128)(2,1)} %all-gather.6.cloned.1.call-done, bf16[576,8192]{1,0:T(8,128)(2,1)} %all-reduce.2.cloned.1.call-done), kind=kOutput, calls=%fused_computation.7 | convolution fusion | flops 10872299520 | bytes 29638656 | tf_op jit(solution)/shard_map/dot_general | solution.py:20
  441.8 0.0 all-gather.10.cloned.1.call-update
  441.9 0.0 all-gather.8.cloned.1.call-start
  441.9 0.5 all-gather.8.cloned.1.call-update
  442.4 0.0 all-gather.14.cloned.1.call-start
  442.5 0.5 all-gather.14.cloned.1.call-update
  443.0 0.0 copy-start
  443.0 0.2 all-gather.12.cloned.1.call-start
  443.3 60.6 %all-gather.10.cloned.1.call-done = bf16[4608,576]{0,1:T(8,128)(2,1)} async-done(((bf16[1152,576]{0,1:T(8,128)(2,1)}), bf16[4608,576]{0,1:T(8,128)(2,1)}) %all-gather.10.cloned.1.call-update) | async-done | bytes 5308432 | tf_op jit(solution)/shard_map/all_gather | solution.py:40
  503.9 102.0 %all-gather.8.cloned.1.call-done = bf16[1152,4608]{0,1:T(8,128)(2,1)} async-done(((bf16[1152,576]{0,1:T(8,128)(2,1)}), bf16[1152,4608]{0,1:T(8,128)(2,1)}) %all-gather.8.cloned.1.call-update) | async-done | bytes 10616848 | tf_op jit(solution)/shard_map/all_gather | solution.py:39
  605.9 13.1 %fusion.2 = bf16[1152,576]{0,1:T(8,128)(2,1)} fusion(bf16[4608,576]{0,1:T(8,128)(2,1)} %all-gather.10.cloned.1.call-done, bf16[1152,4608]{0,1:T(8,128)(2,1)} %all-gather.8.cloned.1.call-done, bf16[1152,576]{0,1:T(8,128)(2,1)} %convolution_convert_fusion), kind=kOutput, calls=%fused_computation.8 | convolution fusion | flops 6118612992 | bytes 18579456 | tf_op jit(solution)/shard_map/dot_general | solution.py:41
  618.9 0.0 all-gather.12.cloned.1.call-update
  619.0 83.1 %all-gather.14.cloned.1.call-done = bf16[4608,1024]{1,0:T(8,128)(2,1)} async-done(((bf16[1152,1024]{1,0:T(8,128)(2,1)}), bf16[4608,1024]{1,0:T(8,128)(2,1)}) %all-gather.14.cloned.1.call-update) | async-done | bytes 9437200 | tf_op jit(solution)/shard_map/all_gather | solution.py:46
  702.1 102.0 %all-gather.12.cloned.1.call-done = bf16[1152,4608]{0,1:T(8,128)(2,1)} async-done(((bf16[1152,576]{0,1:T(8,128)(2,1)}), bf16[1152,4608]{0,1:T(8,128)(2,1)}) %all-gather.12.cloned.1.call-update) | async-done | bytes 10616848 | tf_op jit(solution)/shard_map/all_gather | solution.py:43
  804.1 0.0 copy-done
  804.1 17.5 %fusion = f32[1152,1024]{1,0:T(8,128)} fusion(bf16[1152,4608]{0,1:T(8,128)(2,1)} %all-gather.12.cloned.1.call-done, bf16[4608,1024]{1,0:T(8,128)(2,1)} %all-gather.14.cloned.1.call-done, bf16[1152,1024]{1,0:T(8,128)(2,1)S(1)} %copy-done), kind=kOutput, calls=%fused_computation.2 | convolution fusion | flops 10876354560 | bytes 27131904 | tf_op jit(solution)/shard_map/dot_general | solution.py:44
Async XLA Ops:
  6.5 219.9 %all-gather.6.cloned.1.call-start = ((), (), s32[]{:S(2)}) async-start(), calls=%async_computation | async-start | bytes 21233664 | tf_op jit(solution)/shard_map/all_gather | solution.py:34
  58.0 365.0 %all-reduce.2.cloned.1.call-start = ((), (), s32[]{:S(2)}) async-start(), calls=%async_computation.1 | async-start | bytes 18874368 | tf_op jit(solution)/shard_map/psum | solution.py:16
  236.2 267.6 %all-gather.10.cloned.1.call-start = ((), (), s32[]{:S(2)}) async-start(), calls=%async_computation.3 | async-start | bytes 6635520 | tf_op jit(solution)/shard_map/all_gather | solution.py:40
  441.9 164.0 %all-gather.8.cloned.1.call-start = ((), (), s32[]{:S(2)}) async-start(), calls=%async_computation.2 | async-start | bytes 11943936 | tf_op jit(solution)/shard_map/all_gather | solution.py:39
  442.4 259.7 %all-gather.14.cloned.1.call-start = ((), (), s32[]{:S(2)}) async-start(), calls=%async_computation.5 | async-start | bytes 11796480 | tf_op jit(solution)/shard_map/all_gather | solution.py:46
  443.0 361.1 %copy-start = (bf16[1152,1024]{1,0:T(8,128)(2,1)S(1)}, bf16[1152,1024]{1,0:T(8,128)(2,1)}, u32[]{:S(2)}) copy-start(bf16[1152,1024]{1,0:T(8,128)(2,1)} %multiply_convert_fusion) | copy-start | bytes 7077892
  443.0 361.0 %all-gather.12.cloned.1.call-start = ((), (), s32[]{:S(2)}) async-start(), calls=%async_computation.4 | async-start | bytes 11943936 | tf_op jit(solution)/shard_map/all_gather | solution.py:43
Sparse Core Ops, SparseCore 0:
  58.2 168.2 all-gather.5
  236.4 186.5 all-reduce.1
  442.0 61.8 all-gather.9
  505.4 100.4 all-gather.7
  607.5 94.5 all-gather.13
  703.6 100.4 all-gather.11
where the time goes:
time: 829 us; the launch traced here: 828 us
  waiting for transfers between devices  704 us (85%)
  matrix products  49.4 us (6%)
  blocking collectives  42.2 us (5%)
  other arithmetic  18.3 us (2%)
  between operations  14.2 us (2%)
    psum x1, waiting for transfers between devices, from_root(): return lax.psum(jnp.where(mine, shard, jnp.zeros_like(shard)), axis)  187 us
    all_gather x1, waiting for transfers between devices, body(): row_panel = lax.all_gather(scaled, 'col', axis=1, tiled=True)  168 us
    all_gather x1, waiting for transfers between devices, body(): gram_panel = lax.all_gather(gram, 'col', axis=1, tiled=True)  102 us
    all_gather x1, waiting for transfers between devices, body(): poly_panel = lax.all_gather(poly, 'col', axis=1, tiled=True)  102 us
    all_gather x1, waiting for transfers between devices, body(): lax.all_gather(scaled, 'row', axis=0, tiled=True)  83.1 us
    all_gather x1, waiting for transfers between devices, body(): gram_columns = lax.all_gather(gram, 'row', axis=0, tiled=True)  60.6 us
    psum x1, blocking collectives, body(): norm_squares = lax.psum(partial_sum, ('row', 'col'))  42.2 us
    dot_general x1, matrix products, rows_product(): lax.dot_general(left, right, (((1,), (1,)), ((), ())), preferred_element_...  18.8 us
  transfers between devices with their start and end apart: 6, of which 6 were waited for; matrix products, arithmetic and copies ran while one was open for 2% of the time, Pallas kernels for 0%

commit v1 on v0

--- a/solution.py
+++ b/solution.py
@@ -37,7 +37,13 @@
     peer_rows = from_root(own_part, "row", source_row)
     gram = rows_product(row_panel, peer_rows).astype(jnp.bfloat16)
     gram_panel = lax.all_gather(gram, "col", axis=1, tiled=True)
-    gram_columns = lax.all_gather(gram, "row", axis=0, tiled=True)
+    count = lax.axis_size("row")
+    held, parts = (gram, [gram])
+    for _ in range(count - 1):
+        held = lax.ppermute(held, "row", [(i, (i + 1) % count) for i in range(count)])
+        parts.insert(0, held)
+    flat = jnp.concatenate(parts, axis=0)
+    gram_columns = jnp.roll(flat, (lax.axis_index("row") + 1) * gram.shape[0], axis=0)
     squared = jnp.dot(gram_panel, gram_columns, preferred_element_type=jnp.float32)
     poly = (quintic_b * gram.astype(jnp.float32) + quintic_c * squared).astype(jnp.bfloat16)
     poly_panel = lax.all_gather(poly, "col", axis=1, tiled=True)

time: 829 us -> 765 us (0.923)
  waiting for transfers between devices: 704 us -> 622 us
  local copies, waits for them, and re-layouts: 0.01 us -> 15.2 us
    all_gather x1, waiting for transfers between devices: 102 us -> 0.01 us  [body(): gram_panel = lax.all_gather(gram, 'col', axis=1, tiled=True)]
    ppermute x0 -> x3, waiting for transfers between devices: none -> 91.1 us  [body(): lax.ppermute(held, 'row', [(i, (i + 1) % count) for i in range(count)])]
    all_gather x1 -> x0, waiting for transfers between devices: 60.6 us -> none  [body(): gram_columns = lax.all_gather(gram, 'row', axis=0, tiled=True)]
    unnamed x2 -> x11, local copies, waits for them, and re-layouts: 0.01 us -> 13.9 us
    all_gather x1, waiting for transfers between devices: 83.1 us -> 73.1 us  [body(): lax.all_gather(scaled, 'row', axis=0, tiled=True)]
  transfers between devices with their start and end apart: 6 -> 8, of which waited for: 6 -> 7; matrix products, arithmetic and copies ran while one was open for 2% -> 4% of each run, Pallas kernels for 0% -> 0%
where the time goes in v1:
time: 765 us
  waiting for transfers between devices  622 us (81%)
  matrix products  51 us (7%)
  blocking collectives  42.2 us (6%)
  other arithmetic  18.3 us (2%)
  local copies, waits for them, and re-layouts  15.2 us (2%)
  between operations  13.9 us (2%)
    psum x1, waiting for transfers between devices, from_root(): return lax.psum(jnp.where(mine, shard, jnp.zeros_like(shard)), axis)  187 us
    all_gather x1, waiting for transfers between devices, body(): row_panel = lax.all_gather(scaled, 'col', axis=1, tiled=True)  168 us
    all_gather x1, waiting for transfers between devices, body(): poly_panel = lax.all_gather(poly, 'col', axis=1, tiled=True)  102 us
    ppermute x3, waiting for transfers between devices, body(): lax.ppermute(held, 'row', [(i, (i + 1) % count) for i in range(count)])  91.1 us
    all_gather x1, waiting for transfers between devices, body(): lax.all_gather(scaled, 'row', axis=0, tiled=True)  73.1 us
    psum x1, blocking collectives, body(): norm_squares = lax.psum(partial_sum, ('row', 'col'))  42.2 us
    dot_general x1, matrix products, rows_product(): lax.dot_general(left, right, (((1,), (1,)), ((), ())), preferred_element_...  18.8 us
    dot_general x1, matrix products, body(): jnp.dot(poly_panel, lax.all_gather(scaled, 'row', axis=0, tiled=True), pr...  17.5 us
  transfers between devices with their start and end apart: 8, of which 7 were waited for; matrix products, arithmetic and copies ran while one was open for 4% of the time, Pallas kernels for 0%

profile of v1, /device:TPU:0, one launch (start us, length us, event | category | flops | bytes accessed | tf_op | source)
XLA Modules:
  0.0 764.7 jit_solution(13011157864566619945)
XLA Ops:
  6.5 0.0 all-gather.5.cloned.1.call-start
  6.5 4.2 multiply_reduce_fusion
  10.7 42.2 %psum.14 = f32[]{:T(128)} all-reduce(f32[]{:T(128)} %multiply_reduce_fusion), channel_id=1, replica_groups=mesh['row'=4,'col'=8] {'row','col'}, use_global_device_ids=true, to_apply=%region_1.0 | all-reduce | flops 1 | bytes 8 | tf_op jit(solution)/shard_map/psum | solution.py:27
  53.6 4.4 multiply_convert_fusion
  58.0 0.0 all-gather.5.cloned.1.call-update
  58.0 0.0 all-reduce.2.cloned.1.call-start
  58.1 168.3 %all-gather.5.cloned.1.call-done = bf16[1152,8192]{1,0:T(8,128)(2,1)} async-done(((bf16[1152,1024]{1,0:T(8,128)(2,1)}), bf16[1152,8192]{1,0:T(8,128)(2,1)}) %all-gather.5.cloned.1.call-update) | async-done | bytes 18874384 | tf_op jit(solution)/shard_map/all_gather | solution.py:34
  226.4 9.8 %dynamic-slice_select_fusion = bf16[576,8192]{1,0:T(8,128)(2,1)} fusion(bf16[1152,8192]{1,0:T(8,128)(2,1)} %all-gather.5.cloned.1.call-done, s32[]{:T(128)S(6)} %select_n.37, pred[]{:T(512)S(6)} %eq.8), kind=kLoop, calls=%fused_computation | loop fusion | flops 4718592 | bytes 18874372 | tf_op jit(solution)/shard_map/jit(_where)/select_n | solution.py:16
  236.2 0.0 all-reduce.2.cloned.1.call-update
  236.2 0.0 all-gather.7.cloned.1.call-start
  236.3 186.7 %all-reduce.2.cloned.1.call-done = bf16[576,8192]{1,0:T(8,128)(2,1)} async-done(((bf16[576,8192]{1,0:T(8,128)(2,1)}), bf16[576,8192]{1,0:T(8,128)(2,1)}) %all-reduce.2.cloned.1.call-update) | async-done | bytes 9437200 | tf_op jit(solution)/shard_map/psum | solution.py:16
  423.0 18.8 %convolution_convert_fusion = bf16[1152,576]{0,1:T(8,128)(2,1)} fusion(bf16[1152,8192]{1,0:T(8,128)(2,1)} %all-gather.5.cloned.1.call-done, bf16[576,8192]{1,0:T(8,128)(2,1)} %all-reduce.2.cloned.1.call-done), kind=kOutput, calls=%fused_computation.10 | convolution fusion | flops 10872299520 | bytes 29638656 | tf_op jit(solution)/shard_map/dot_general | solution.py:20
  441.8 0.0 copy-start.1
  441.8 0.0 all-gather.7.cloned.1.call-update
  441.8 0.0 all-gather.11.cloned.1.call-start
  441.8 0.5 all-gather.11.cloned.1.call-update
  442.4 0.0 all-gather.9.cloned.1.call-start
  442.4 1.5 collective-permute-start
  443.9 30.4 %collective-permute-done = bf16[1152,576]{0,1:T(8,128)(2,1)S(1)} collective-permute-done((bf16[1152,576]{0,1:T(8,128)(2,1)}, bf16[1152,576]{0,1:T(8,128)(2,1)S(1)}, u32[]{:S(2)}, u32[]{:S(2)}) %collective-permute-start) | collective-permute-done | bytes 1327136 | tf_op jit(solution)/shard_map/ppermute | solution.py:43
  474.3 0.6 collective-permute-start.1
  474.9 30.4 %collective-permute-done.1 = bf16[1152,576]{0,1:T(8,128)(2,1)} collective-permute-done((bf16[1152,576]{0,1:T(8,128)(2,1)S(1)}, bf16[1152,576]{0,1:T(8,128)(2,1)}, u32[]{:S(2)}, u32[]{:S(2)}) %collective-permute-start.1) | collective-permute-done | bytes 1327136 | tf_op jit(solution)/shard_map/ppermute | solution.py:43
  505.3 0.0 collective-permute-start.2
  505.3 30.3 %collective-permute-done.2 = bf16[1152,576]{0,1:T(8,128)(2,1)} collective-permute-done((bf16[1152,576]{0,1:T(8,128)(2,1)}, bf16[1152,576]{0,1:T(8,128)(2,1)}, u32[]{:S(2)}, u32[]{:S(2)}) %collective-permute-start.2) | collective-permute-done | bytes 1327136 | tf_op jit(solution)/shard_map/ppermute | solution.py:43
  535.6 2.6 constant_dynamic-update-slice_fusion.7
  538.2 2.5 constant_dynamic-update-slice_fusion.6
  540.7 1.3 constant_dynamic-update-slice_fusion.5
  542.0 0.0 copy-done.1
  542.0 1.2 constant_dynamic-update-slice_fusion.4
  543.3 2.5 constant_dynamic-update-slice_fusion.3
  545.8 2.5 constant_dynamic-update-slice_fusion.2
  548.3 1.2 constant_dynamic-update-slice_fusion.1
  549.5 1.2 constant_dynamic-update-slice_fusion
  550.8 0.0 copy-start
  550.8 0.0 all-gather.7.cloned.1.call-done
  550.8 14.7 %fusion.9 = bf16[1152,576]{0,1:T(8,128)(2,1)} fusion(bf16[1152,4608]{0,1:T(8,128)(2,1)} %all-gather.7.cloned.1.call-done, bf16[9216,576]{0,1:T(8,128)(2,1)} %constant_dynamic-update-slice_fusion, s32[]{:T(128)S(6)} %select_n.40, bf16[1152,576]{0,1:T(8,128)(2,1)} %convolution_convert_fusion), kind=kOutput, calls=%fused_computation.9 | convolution fusion | flops 6118612992 | bytes 18579460 | tf_op jit(solution)/shard_map/dot_general | solution.py:47
  565.5 0.0 all-gather.9.cloned.1.call-update
  565.5 73.1 %all-gather.11.cloned.1.call-done = bf16[4608,1024]{1,0:T(8,128)(2,1)} async-done(((bf16[1152,1024]{1,0:T(8,128)(2,1)}), bf16[4608,1024]{1,0:T(8,128)(2,1)}) %all-gather.11.cloned.1.call-update) | async-done | bytes 9437200 | tf_op jit(solution)/shard_map/all_gather | solution.py:52
  638.7 102.0 %all-gather.9.cloned.1.call-done = bf16[1152,4608]{0,1:T(8,128)(2,1)} async-done(((bf16[1152,576]{0,1:T(8,128)(2,1)}), bf16[1152,4608]{0,1:T(8,128)(2,1)}) %all-gather.9.cloned.1.call-update) | async-done | bytes 10616848 | tf_op jit(solution)/shard_map/all_gather | solution.py:49
  740.7 0.0 copy-done
  740.7 17.5 %fusion.2 = f32[1152,1024]{1,0:T(8,128)} fusion(bf16[1152,4608]{0,1:T(8,128)(2,1)} %all-gather.9.cloned.1.call-done, bf16[4608,1024]{1,0:T(8,128)(2,1)} %all-gather.11.cloned.1.call-done, bf16[1152,1024]{1,0:T(8,128)(2,1)S(1)} %copy-done), kind=kOutput, calls=%fused_computation.4 | convolution fusion | flops 10876354560 | bytes 27131904 | tf_op jit(solution)/shard_map/dot_general | solution.py:50
Async XLA Ops:
  6.5 219.9 %all-gather.5.cloned.1.call-start = ((), (), s32[]{:S(2)}) async-start(), calls=%async_computation | async-start | bytes 21233664 | tf_op jit(solution)/shard_map/all_gather | solution.py:34
  58.0 365.0 %all-reduce.2.cloned.1.call-start = ((), (), s32[]{:S(2)}) async-start(), calls=%async_computation.1 | async-start | bytes 18874368 | tf_op jit(solution)/shard_map/psum | solution.py:16
  236.2 314.5 %all-gather.7.cloned.1.call-start = ((), (), s32[]{:S(2)}) async-start(), calls=%async_computation.2 | async-start | bytes 11943936 | tf_op jit(solution)/shard_map/all_gather | solution.py:39
  441.8 100.3 %copy-start.1 = (bf16[1152,576]{0,1:T(8,128)(2,1)S(1)}, bf16[1152,576]{0,1:T(8,128)(2,1)}, u32[]{:S(2)}) copy-start(bf16[1152,576]{0,1:T(8,128)(2,1)} %convolution_convert_fusion) | copy-start | bytes 3981316
  441.8 196.9 %all-gather.11.cloned.1.call-start = ((), (), s32[]{:S(2)}) async-start(), calls=%async_computation.4 | async-start | bytes 11796480 | tf_op jit(solution)/shard_map/all_gather | solution.py:52
  442.4 298.3 %all-gather.9.cloned.1.call-start = ((), (), s32[]{:S(2)}) async-start(), calls=%async_computation.3 | async-start | bytes 11943936 | tf_op jit(solution)/shard_map/all_gather | solution.py:49
  442.4 31.9 %collective-permute-start = (bf16[1152,576]{0,1:T(8,128)(2,1)}, bf16[1152,576]{0,1:T(8,128)(2,1)S(1)}, u32[]{:S(2)}, u32[]{:S(2)}) collective-permute-start(bf16[1152,576]{0,1:T(8,128)(2,1)} %convolution_convert_fusion), channel_id=1, source_target_pairs={{0,8},{8,16},{16,24},{24,0},{1,9},{9,17},{17,25},{25,1},{2,10},{10... | collective-permute-start | bytes 3981320 | tf_op jit(solution)/shard_map/ppermute | solution.py:43
  474.3 31.0 %collective-permute-start.1 = (bf16[1152,576]{0,1:T(8,128)(2,1)S(1)}, bf16[1152,576]{0,1:T(8,128)(2,1)}, u32[]{:S(2)}, u32[]{:S(2)}) collective-permute-start(bf16[1152,576]{0,1:T(8,128)(2,1)S(1)} %collective-permute-done), channel_id=1, source_target_pairs={{0,8},{8,16},{16,24},{24,0},{1,9},{9,17},{17,25},{25,1},{2,10},{10... | collective-permute-start | bytes 3981320 | tf_op jit(solution)/shard_map/ppermute | solution.py:43
  505.3 30.3 %collective-permute-start.2 = (bf16[1152,576]{0,1:T(8,128)(2,1)}, bf16[1152,576]{0,1:T(8,128)(2,1)}, u32[]{:S(2)}, u32[]{:S(2)}) collective-permute-start(bf16[1152,576]{0,1:T(8,128)(2,1)} %collective-permute-done.1), channel_id=1, source_target_pairs={{0,8},{8,16},{16,24},{24,0},{1,9},{9,17},{17,25},{25,1},{2,10},{10... | collective-permute-start | bytes 3981320 | tf_op jit(solution)/shard_map/ppermute | solution.py:43
  550.8 189.9 %copy-start = (bf16[1152,1024]{1,0:T(8,128)(2,1)S(1)}, bf16[1152,1024]{1,0:T(8,128)(2,1)}, u32[]{:S(2)}) copy-start(bf16[1152,1024]{1,0:T(8,128)(2,1)} %multiply_convert_fusion) | copy-start | bytes 7077892
Sparse Core Ops, SparseCore 0:
  58.1 168.2 all-gather.4
  236.3 186.5 all-reduce.1
  441.9 100.4 all-gather.6
  544.1 94.5 all-gather.10
  640.2 100.4 all-gather.8
